TPU v7x, 32 devices: a whole 2x2x4 slice. The times are simulated.
32 devices in a mesh: ctx: 8 (over z, x), ch: 4 (over y, core).
Axes of the slice: x: 2, y: 2, z: 4, core: 2. Of those that a mesh axis runs over, the one named last changes fastest.
Arguments:
- conv_input: bfloat16 [128, 1024], P('ch', 'ctx'), may hold values from -6 to 6
- gate_value: bfloat16 [128, 1024], P('ch', 'ctx'), may hold values from -6 to 6
- out_grad: bfloat16 [128, 1024], P('ch', 'ctx'), may hold values from -6 to 6
- long_filter: bfloat16 [128, 1024], P('ch', 'ctx'), may hold values from -4 to 4
- skip_bias: float32 [128], P('ch'), may hold values from 0.5 to 1.5
- short_weight: float32 [128, 3], P('ch'), may hold values from -3.5 to 3.5
Outputs:
- input_grad: bfloat16 [128, 1024], P('ch', 'ctx')
- filter_grad: float32 [128, 1024], P('ch', 'ctx')
All inputs are finite; a program needn't handle non-finite values.
Results may differ from a plain program's by a relative error of at most 0.007.
Values may be sent and summed in bfloat16 or wider, within the bound.
A program may use at most 64 MiB of HBM per device.

v0:
```python
import math

import jax
import jax.numpy as jnp
from jax import lax
from jax.sharding import PartitionSpec as P


def from_behind(value, axis, steps):
    count = lax.axis_size(axis)
    initial, last = (max(0, -steps), min(count, count - steps))
    return lax.ppermute(value, axis, [(source, source + steps) for source in range(initial, last)])


def packed_tables(block_len):
    span_len = 2 * block_len
    sample_idx = jnp.arange(span_len, dtype=jnp.int32)[:, None]
    freq_idx = jnp.arange(block_len + 1, dtype=jnp.int32)[None, :]
    angle_fwd = 2.0 * math.pi / span_len * (sample_idx * freq_idx % span_len).astype(jnp.float32)
    forward = jnp.concatenate([jnp.cos(angle_fwd), -jnp.sin(angle_fwd[:, 1:block_len])], axis=1)
    column_idx = jnp.arange(span_len, dtype=jnp.int32)[None, :]
    real_freq = jnp.arange(block_len + 1, dtype=jnp.int32)[:, None]
    real_weight = jnp.where((real_freq == 0) | (real_freq == block_len), 1.0, 2.0) / span_len
    angle_real = 2.0 * math.pi / span_len * (real_freq * column_idx % span_len).astype(jnp.float32)
    imag_freq = jnp.arange(1, block_len, dtype=jnp.int32)[:, None]
    angle_imag = 2.0 * math.pi / span_len * (imag_freq * column_idx % span_len).astype(jnp.float32)
    inverse = jnp.concatenate(
        [real_weight * jnp.cos(angle_real), -2.0 / span_len * jnp.sin(angle_imag)], axis=0
    )
    return (forward, inverse)


def split_table(table):
    upper = table.astype(jnp.bfloat16)
    lower = (table - upper.astype(jnp.float32)).astype(jnp.bfloat16)
    return (upper, lower)


def split_dot(data, parts):
    return jnp.dot(data, parts[0], preferred_element_type=jnp.float32) + jnp.dot(
        data, parts[1], preferred_element_type=jnp.float32
    )


def conj_times(first, second, block_len):
    zero_col = jnp.zeros(first.shape[:-1] + (1,), jnp.float32)
    first_re = first[..., : block_len + 1]
    first_im = jnp.concatenate([zero_col, first[..., block_len + 1 :], zero_col], axis=-1)
    second_re = second[..., : block_len + 1]
    second_im = jnp.concatenate([zero_col, second[..., block_len + 1 :], zero_col], axis=-1)
    prod_re = first_re * second_re + first_im * second_im
    prod_im = first_re * second_im - first_im * second_re
    return jnp.concatenate([prod_re, prod_im[..., 1:block_len]], axis=-1)


def spectral_dot(left, right):
    return jnp.dot(left, right, precision=lax.Precision.HIGH, preferred_element_type=jnp.float32)


def per_device(conv_input, gate_value, out_grad, long_filter, skip_bias, short_weight):
    channels = conv_input.shape[0]
    block_len = conv_input.shape[1]
    span_len = 2 * block_len
    shards = lax.axis_size("ctx")
    own_index = lax.axis_index("ctx")
    forward, inverse = packed_tables(block_len)
    forward_parts = split_table(forward)
    head_parts = split_table(forward[:block_len])
    conv_grad = (gate_value.astype(jnp.float32) * out_grad.astype(jnp.float32)).astype(jnp.bfloat16)
    whole_filter = lax.all_gather(long_filter, "ctx", axis=1, tiled=True)
    padded_filter = jnp.concatenate(
        [jnp.zeros((channels, block_len), jnp.bfloat16), whole_filter], axis=1
    )

    def mid_term(grad_block, block_idx):
        first_col = jnp.clip(block_idx - own_index, 0, shards - 1) * block_len
        segment = lax.dynamic_slice_in_dim(padded_filter, first_col, span_len, 1)
        grad_spec = split_dot(grad_block, head_parts)
        filter_spec = split_dot(segment, forward_parts)
        return (grad_spec, conj_times(grad_spec, filter_spec, block_len), first_col)

    own_spec = split_dot(conv_input, head_parts)
    roll_table = jnp.concatenate([inverse[:, block_len:], inverse[:, :block_len]], axis=1)

    def add_block(state, grad_block, block_idx):
        mid_acc, lag_acc = state
        grad_spec, mid_piece, first_col = mid_term(grad_block, block_idx)
        lag_piece = spectral_dot(conj_times(own_spec, grad_spec, block_len), roll_table)
        previous = lax.dynamic_slice_in_dim(lag_acc, first_col, span_len, 1)
        lag_acc = lax.dynamic_update_slice_in_dim(lag_acc, previous + lag_piece, first_col, 1)
        return (mid_acc + mid_piece, lag_acc)

    init_state = (
        jnp.zeros((channels, span_len), jnp.float32),
        jnp.zeros((channels, shards * block_len + block_len), jnp.float32),
    )
    piece = lax.all_gather(conv_grad, "ctx", axis=1, tiled=True)
    blocks_in = piece.shape[1] // block_len
    stacked = jnp.moveaxis(piece.reshape(channels, blocks_in, block_len), 1, 0)
    indices = jnp.arange(blocks_in, dtype=jnp.int32)

    def step_one(carry, item):
        grad_block, block_idx = item
        result = lax.cond(
            block_idx >= own_index,
            lambda inner: add_block(inner, grad_block, block_idx),
            lambda inner: inner,
            carry,
        )
        return (result, None)

    result, unused = lax.scan(step_one, init_state, (stacked, indices))
    mid_acc, lag_acc = result
    lag_part = lag_acc[:, block_len:] * (1.0 / math.sqrt(shards * block_len))
    filter_grad = lax.psum_scatter(lag_part, "ctx", scatter_dimension=1, tiled=True)
    mid_table = inverse[:, 1 : block_len + 1][:, ::-1]
    mid_grad = (
        spectral_dot(mid_acc, mid_table) + skip_bias[:, None] * conv_grad.astype(jnp.float32)
    ).astype(jnp.bfloat16)
    taps = short_weight.shape[1]
    edge_rows = from_behind(mid_grad[:, : taps - 1], "ctx", -1)
    extended = jnp.concatenate([mid_grad, edge_rows], axis=1).astype(jnp.float32)
    input_grad = jnp.zeros((channels, block_len), jnp.float32)
    for tap_index in range(taps):
        input_grad = (
            input_grad
            + short_weight[:, tap_index : tap_index + 1]
            * extended[:, tap_index : tap_index + block_len]
        )
    return (input_grad.astype(jnp.bfloat16), filter_grad)


def solution(mesh):
    placed = (
        P("ch", "ctx"),
        P("ch", "ctx"),
        P("ch", "ctx"),
        P("ch", "ctx"),
        P("ch"),
        P("ch", None),
    )
    return jax.shard_map(
        per_device,
        mesh=mesh,
        in_specs=placed,
        out_specs=(P("ch", "ctx"), P("ch", "ctx")),
        check_vma=False,
    )
```

profile of v0, /device:TPU:0, one launch (start us, length us, event | category | flops | bytes accessed | tf_op | source)
XLA Modules:
  0.0 163.9 jit_solution(6427294845297295743)
XLA Ops:
  7.4 1.0 fusion.48
  8.3 0.5 fusion.44
  9.1 0.5 fusion.32
  9.6 0.6 fusion.40
  10.3 27.7 %all_gather.6 = bf16[32,1024]{1,0:T(8,128)(2,1)S(1)} all-gather(bf16[32,128]{1,0:T(8,128)(2,1)S(1)} %multiply_convert_fusion), channel_id=1, replica_groups=mesh['ctx'=8,'ch'=4] {'ctx'}, dimensions={1}, use_global_device_ids=true | all-gather | bytes 73728 | tf_op jit(solution)/shard_map/all_gather | solution.py:97
  38.1 0.7 copy-done.3
  38.8 26.0 %all_gather.7 = bf16[32,1024]{1,0:T(8,128)(2,1)S(1)} all-gather(bf16[32,128]{1,0:T(8,128)(2,1)S(1)} %copy-done.3), channel_id=1, replica_groups=mesh['ctx'=8,'ch'=4] {'ctx'}, dimensions={1}, use_global_device_ids=true | all-gather | bytes 73728 | tf_op jit(solution)/shard_map/all_gather | solution.py:70
  65.3 28.0 %while.12 = (s32[]{:T(128)}, f32[32,256]{1,0:T(8,128)S(1)}, f32[32,1152]{1,0:T(8,128)S(1)}, s32[8]{0:T(128)S(1)}, s32[]{:T(128)}, /*index=5*/bf16[8,32,128]{2,1,...) while((s32[]{:T(128)}, f32[32,256]{1,0:T(8,128)S(1)}, ...), condition=%wide.region_3.4_spmd, body=%wide.region_0.3_spmd.sunk | while | flops 25305420 | bytes 1605401 | solution.py:112
  65.3 0.7 dynamic_slice.32
  66.6 2.1 %conditional.2 = ((f32[32,256]{1,0:T(8,128)S(1)}, f32[32,1152]{1,0:T(8,128)S(1)})) conditional(s32[]{:T(128)} %convert_element_type.104, (f32[32,256]{1,0:T(8,128)S(1)}, f32[32,1152]{1,0:T(8,128)S(1)}) %tuple.47, (bf16[8,32,128]{2,1,0:T(8,128)(2,1)S(1)}, s32[]{:T(128)}, bf16[128,256]{1,0:T(8,128)(2,1)S(1)}, bf16[128,256]{1,0:T(8,128)(2,1)S(1)}, ...), branch_computations={%region_1.1_spmd, %region_2.2_spmd} | conditional | flops 25305416 | bytes 1605122 | solution.py:104
  68.8 0.7 dynamic_slice.32
  70.1 2.1 %conditional.2 = ((f32[32,256]{1,0:T(8,128)S(1)}, f32[32,1152]{1,0:T(8,128)S(1)})) conditional(s32[]{:T(128)} %convert_element_type.104, (f32[32,256]{1,0:T(8,128)S(1)}, f32[32,1152]{1,0:T(8,128)S(1)}) %tuple.47, (bf16[8,32,128]{2,1,0:T(8,128)(2,1)S(1)}, s32[]{:T(128)}, bf16[128,256]{1,0:T(8,128)(2,1)S(1)}, bf16[128,256]{1,0:T(8,128)(2,1)S(1)}, ...), branch_computations={%region_1.1_spmd, %region_2.2_spmd} | conditional | flops 25305416 | bytes 1605122 | solution.py:104
  71.9 0.2 fusion
  72.3 0.7 dynamic_slice.32
  73.6 2.1 %conditional.2 = ((f32[32,256]{1,0:T(8,128)S(1)}, f32[32,1152]{1,0:T(8,128)S(1)})) conditional(s32[]{:T(128)} %convert_element_type.104, (f32[32,256]{1,0:T(8,128)S(1)}, f32[32,1152]{1,0:T(8,128)S(1)}) %tuple.47, (bf16[8,32,128]{2,1,0:T(8,128)(2,1)S(1)}, s32[]{:T(128)}, bf16[128,256]{1,0:T(8,128)(2,1)S(1)}, bf16[128,256]{1,0:T(8,128)(2,1)S(1)}, ...), branch_computations={%region_1.1_spmd, %region_2.2_spmd} | conditional | flops 25305416 | bytes 1605122 | solution.py:104
  75.8 0.7 dynamic_slice.32
  77.1 2.1 %conditional.2 = ((f32[32,256]{1,0:T(8,128)S(1)}, f32[32,1152]{1,0:T(8,128)S(1)})) conditional(s32[]{:T(128)} %convert_element_type.104, (f32[32,256]{1,0:T(8,128)S(1)}, f32[32,1152]{1,0:T(8,128)S(1)}) %tuple.47, (bf16[8,32,128]{2,1,0:T(8,128)(2,1)S(1)}, s32[]{:T(128)}, bf16[128,256]{1,0:T(8,128)(2,1)S(1)}, bf16[128,256]{1,0:T(8,128)(2,1)S(1)}, ...), branch_computations={%region_1.1_spmd, %region_2.2_spmd} | conditional | flops 25305416 | bytes 1605122 | solution.py:104
  79.3 0.7 dynamic_slice.32
  80.6 2.1 %conditional.2 = ((f32[32,256]{1,0:T(8,128)S(1)}, f32[32,1152]{1,0:T(8,128)S(1)})) conditional(s32[]{:T(128)} %convert_element_type.104, (f32[32,256]{1,0:T(8,128)S(1)}, f32[32,1152]{1,0:T(8,128)S(1)}) %tuple.47, (bf16[8,32,128]{2,1,0:T(8,128)(2,1)S(1)}, s32[]{:T(128)}, bf16[128,256]{1,0:T(8,128)(2,1)S(1)}, bf16[128,256]{1,0:T(8,128)(2,1)S(1)}, ...), branch_computations={%region_1.1_spmd, %region_2.2_spmd} | conditional | flops 25305416 | bytes 1605122 | solution.py:104
  82.8 0.7 dynamic_slice.32
  84.1 2.1 %conditional.2 = ((f32[32,256]{1,0:T(8,128)S(1)}, f32[32,1152]{1,0:T(8,128)S(1)})) conditional(s32[]{:T(128)} %convert_element_type.104, (f32[32,256]{1,0:T(8,128)S(1)}, f32[32,1152]{1,0:T(8,128)S(1)}) %tuple.47, (bf16[8,32,128]{2,1,0:T(8,128)(2,1)S(1)}, s32[]{:T(128)}, bf16[128,256]{1,0:T(8,128)(2,1)S(1)}, bf16[128,256]{1,0:T(8,128)(2,1)S(1)}, ...), branch_computations={%region_1.1_spmd, %region_2.2_spmd} | conditional | flops 25305416 | bytes 1605122 | solution.py:104
  86.3 0.7 dynamic_slice.32
  87.6 2.1 %conditional.2 = ((f32[32,256]{1,0:T(8,128)S(1)}, f32[32,1152]{1,0:T(8,128)S(1)})) conditional(s32[]{:T(128)} %convert_element_type.104, (f32[32,256]{1,0:T(8,128)S(1)}, f32[32,1152]{1,0:T(8,128)S(1)}) %tuple.47, (bf16[8,32,128]{2,1,0:T(8,128)(2,1)S(1)}, s32[]{:T(128)}, bf16[128,256]{1,0:T(8,128)(2,1)S(1)}, bf16[128,256]{1,0:T(8,128)(2,1)S(1)}, ...), branch_computations={%region_1.1_spmd, %region_2.2_spmd} | conditional | flops 25305416 | bytes 1605122 | solution.py:104
  89.7 0.7 dynamic_slice.32
  91.1 2.1 %conditional.2 = ((f32[32,256]{1,0:T(8,128)S(1)}, f32[32,1152]{1,0:T(8,128)S(1)})) conditional(s32[]{:T(128)} %convert_element_type.104, (f32[32,256]{1,0:T(8,128)S(1)}, f32[32,1152]{1,0:T(8,128)S(1)}) %tuple.47, (bf16[8,32,128]{2,1,0:T(8,128)(2,1)S(1)}, s32[]{:T(128)}, bf16[128,256]{1,0:T(8,128)(2,1)S(1)}, bf16[128,256]{1,0:T(8,128)(2,1)S(1)}, ...), branch_computations={%region_1.1_spmd, %region_2.2_spmd} | conditional | flops 25305416 | bytes 1605122 | solution.py:104
  93.4 0.7 copy-done.5
  94.2 1.3 collective-permute-start
  95.5 0.7 slice_multiply_fusion.4
  96.3 0.7 copy-done.4
  96.9 2.9 %collective-permute-done = bf16[32,2]{1,0:T(8,128)(2,1)S(1)} collective-permute-done((bf16[32,2]{1,0:T(8,128)(2,1)S(1)}, bf16[32,2]{1,0:T(8,128)(2,1)S(1)}, u32[]{:S(2)}, u32[]{:S(2)}) %collective-permute-start) | collective-permute-done | bytes 160 | tf_op jit(solution)/shard_map/ppermute | solution.py:12
  99.8 0.7 fusion.50
  100.5 56.6 %reduce-scatter.2.cloned.1.call-done = f32[32,128]{1,0:T(8,128)} async-done(((f32[32,1024]{1,0:T(8,128)}), f32[32,128]{1,0:T(8,128)}) %reduce-scatter.2.cloned.1.call-update) | async-done | bytes 16400 | tf_op jit(solution)/shard_map/reduce_scatter | solution.py:115
  (133 shorter events, 12.3 us)
Async XLA Ops:
  7.2 57.6 %copy-start = (bf16[32,128]{1,0:T(8,128)(2,1)S(1)}, bf16[32,128]{1,0:T(8,128)(2,1)}, u32[]{:S(2)}) copy-start(bf16[32,128]{1,0:T(8,128)(2,1)} %param.10) | copy-start | bytes 24580
  7.2 149.9 %reduce-scatter.2.cloned.1.call-start = ((), (), s32[]{:S(2)}) async-start(), calls=%async_computation.1 | async-start | bytes 147456 | tf_op jit(solution)/shard_map/reduce_scatter | solution.py:115
  9.6 0.7 copy-start.1
  9.6 0.7 copy-start.2
  38.1 0.7 copy-start.3
  93.4 0.7 copy-start.5
  94.2 5.5 %collective-permute-start = (bf16[32,2]{1,0:T(8,128)(2,1)S(1)}, bf16[32,2]{1,0:T(8,128)(2,1)S(1)}, u32[]{:S(2)}, u32[]{:S(2)}) collective-permute-start(bf16[32,2]{1,0:T(8,128)(2,1)S(1)} %bitcast.35), channel_id=1, source_target_pairs={{4,0},{8,4},{12,8},{16,12},{20,16},{24,20},{28,24},{5,1},{9,5},{13... | collective-permute-start | bytes 392 | tf_op jit(solution)/shard_map/ppermute | solution.py:12
  96.2 0.7 copy-start.4
Sparse Core Ops, SparseCore 0:
  96.4 60.6 reduce-scatter.1
where the time goes:
time: 164 us
  waiting for transfers between devices  59.5 us (36%)
  blocking collectives  53.7 us (33%)
  between operations  14.2 us (9%)
  loops' own time  11.5 us (7%)
  local copies, waits for them, and re-layouts  9.46 us (6%)
  other arithmetic  7.38 us (4%)
  matrix products  6.9 us (4%)
    reduce_scatter x1, waiting for transfers between devices, per_device(): lax.psum_scatter(lag_part, 'ctx', scatter_dimension=1, tiled=True)  56.6 us
    all_gather x1, blocking collectives, per_device(): piece = lax.all_gather(conv_grad, 'ctx', axis=1, tiled=True)  27.7 us
    all_gather x1, blocking collectives, per_device(): whole_filter = lax.all_gather(long_filter, 'ctx', axis=1, tiled=True)  26 us
    another operation x8, loops' own time, step_one(): lax.cond(block_idx >= own_index, lambda inner: add_block(inner, grad_bloc...  5.92 us
    another operation x1, loops' own time, per_device(): result, unused = lax.scan(step_one, init_state, (stacked, indices))  5.57 us
    dynamic_slice x8, local copies, waits for them, and re-layouts, per_device(): result, unused = lax.scan(step_one, init_state, (stacked, indices))  5.29 us
  transfers between devices with their start and end apart: 2, of which 2 were waited for; matrix products, arithmetic and copies ran while one was open for 1% of the time, Pallas kernels for 0%

commit v1 on v0

--- a/solution.py
+++ b/solution.py
@@ -1,8 +1,11 @@
+import functools
 import math
 
 import jax
 import jax.numpy as jnp
 from jax import lax
+from jax.experimental import pallas as pl
+from jax.experimental.pallas import tpu as pltpu
 from jax.sharding import PartitionSpec as P
 
 
@@ -57,7 +60,7 @@
     return jnp.dot(left, right, precision=lax.Precision.HIGH, preferred_element_type=jnp.float32)
 
 
-def per_device(conv_input, gate_value, out_grad, long_filter, skip_bias, short_weight):
+def general_device(conv_input, gate_value, out_grad, long_filter, skip_bias, short_weight):
     channels = conv_input.shape[0]
     block_len = conv_input.shape[1]
     span_len = 2 * block_len
@@ -130,6 +133,211 @@
     return (input_grad.astype(jnp.bfloat16), filter_grad)
 
 
+LANES = 128
+SUBLANES = 8
+
+
+def exchange_kernel(
+    shards,
+    input_ref,
+    gate_ref,
+    grad_ref,
+    filter_ref,
+    skip_ref,
+    short_ref,
+    input_grad_ref,
+    filter_grad_ref,
+    local,
+    send_in,
+    recv_in,
+    rows,
+    products,
+    send_out,
+    recv_out,
+    load_sem,
+    send_in_sem,
+    recv_in_sem,
+    send_out_sem,
+    recv_out_sem,
+):
+    me = lax.axis_index("ctx")
+    channels = local.shape[1]
+    owned = channels // shards
+    taps = short_ref.shape[0]
+    scale = 1.0 / math.sqrt(shards * LANES)
+
+    loads = [
+        pltpu.make_async_copy(source, local.at[slot], load_sem.at[slot])
+        for slot, source in enumerate((gate_ref, grad_ref, filter_ref, input_ref))
+    ]
+    for load in loads:
+        load.start()
+    barrier = pltpu.get_barrier_semaphore()
+    for step in range(1, shards):
+        pl.semaphore_signal(
+            barrier,
+            inc=1,
+            device_id={"ctx": lax.rem(me + step, shards)},
+            device_id_type=pl.DeviceIdType.MESH,
+        )
+    products[:, :, shards * SUBLANES :, :] = jnp.zeros(
+        products.shape[:2] + (products.shape[2] - shards * SUBLANES, LANES), jnp.float32
+    )
+    for load in loads:
+        load.wait()
+
+    lane = lax.broadcasted_iota(jnp.int32, (LANES, LANES), 1)
+    depth = lax.broadcasted_iota(jnp.int32, (LANES, LANES), 0)
+
+    mirror = jnp.where(lane + depth == LANES - 1, 1.0, 0.0).astype(jnp.bfloat16)
+    conv_grad = local[0].astype(jnp.float32) * local[1].astype(jnp.float32)
+    filter_rows = jnp.dot(local[2], mirror, preferred_element_type=jnp.float32)
+    input_rows = jnp.dot(local[3], mirror, preferred_element_type=jnp.float32)
+    for peer in range(shards):
+        own = slice(peer * owned, (peer + 1) * owned)
+        tile = [conv_grad[own], filter_rows[own], input_rows[own]]
+        tile.append(jnp.zeros((send_in.shape[1] - 3 * owned, LANES), jnp.float32))
+        send_in[peer] = jnp.concatenate(tile, axis=0).astype(jnp.bfloat16)
+
+    def sending(send, recv, send_sem, recv_sem, step):
+        peer = lax.rem(me + step, shards)
+        return pltpu.make_async_remote_copy(
+            src_ref=send.at[peer],
+            dst_ref=recv.at[me],
+            send_sem=send_sem.at[step],
+            recv_sem=recv_sem.at[step],
+            device_id={"ctx": peer},
+            device_id_type=pl.DeviceIdType.MESH,
+        )
+
+    def arriving(send, recv, send_sem, recv_sem, step):
+        peer = lax.rem(me + shards - step, shards)
+        return pltpu.make_async_remote_copy(
+            src_ref=send.at[peer],
+            dst_ref=recv.at[peer],
+            send_sem=send_sem.at[step],
+            recv_sem=recv_sem.at[step],
+            device_id={"ctx": peer},
+            device_id_type=pl.DeviceIdType.MESH,
+        )
+
+    first = (send_in, recv_in, send_in_sem, recv_in_sem)
+    second = (send_out, recv_out, send_out_sem, recv_out_sem)
+
+    pl.semaphore_wait(barrier, shards - 1)
+    for step in range(1, shards):
+        sending(*first, step).start()
+    recv_in[me] = send_in[me]
+    for step in range(1, shards):
+        arriving(*first, step).wait_recv()
+    rows[...] = recv_in[...].astype(jnp.float32)
+
+    inside = lane <= depth
+    edge = lax.broadcasted_iota(jnp.int32, (shards, LANES), 1)
+    block = lax.broadcasted_iota(jnp.int32, (shards, LANES), 0)
+    for slot in range(owned):
+        weights = jnp.concatenate(
+            [rows[:, owned + slot, :], rows[:, 2 * owned + slot, :]], axis=0
+        ).astype(jnp.bfloat16)
+        turned = []
+        for part in range(shards):
+            whole = jnp.broadcast_to(rows[part, slot : slot + 1, :], (LANES, LANES))
+            turned.append(pltpu.roll(whole, 1, 1, stride=1, stride_axis=0))
+        turned.append(jnp.zeros((LANES, LANES), jnp.float32))
+        hankel = jnp.concatenate(
+            [
+                jnp.where(inside, turned[part], turned[part + 1]).astype(jnp.bfloat16)
+                for part in range(shards)
+            ],
+            axis=1,
+        )
+        product = jnp.dot(weights, hankel, preferred_element_type=jnp.float32)
+        for part in range(shards):
+            piece = product[:, part * LANES : (part + 1) * LANES]
+            at = slice(part * SUBLANES, (part + 1) * SUBLANES)
+            products[slot, 0, at, :] = piece[:shards]
+            products[slot, 1, at, :] = piece[shards:]
+
+        def gathered(which):
+            total = products[slot, which, pl.ds(0, shards, stride=SUBLANES), :]
+            for part in range(1, shards):
+                total = total + products[
+                    slot, which, pl.ds(part * (SUBLANES + 1), shards, stride=SUBLANES), :
+                ]
+            return total
+
+        channel = me * owned + slot
+        mid = gathered(0) + skip_ref[channel] * rows[:, slot, :]
+        mid = mid.astype(jnp.bfloat16).astype(jnp.float32)
+        total = short_ref[0, channel] * mid
+        for tap in range(1, taps):
+            ahead = pltpu.roll(mid, LANES - tap, 1)
+            carried = jnp.where(block < shards - 1, pltpu.roll(ahead, shards - 1, 0), 0.0)
+            total = total + short_ref[tap, channel] * jnp.where(
+                edge < LANES - tap, ahead, carried
+            )
+        send_out[:, slot, :] = total
+        send_out[:, owned + slot, :] = gathered(1) * scale
+
+    for step in range(1, shards):
+        sending(*second, step).start()
+    recv_out[me] = send_out[me]
+    for step in range(1, shards):
+        arriving(*second, step).wait_recv()
+    for peer in range(0, shards, 2):
+        at = slice(peer * owned, (peer + 2) * owned)
+        input_grad_ref[at, :] = jnp.concatenate(
+            [recv_out[peer, :owned], recv_out[peer + 1, :owned]], axis=0
+        ).astype(jnp.bfloat16)
+        filter_grad_ref[at, :] = jnp.concatenate(
+            [recv_out[peer, owned:], recv_out[peer + 1, owned:]], axis=0
+        )
+    for step in range(1, shards):
+        sending(*first, step).wait_send()
+        sending(*second, step).wait_send()
+
+
+def exchange_device(conv_input, gate_value, out_grad, long_filter, skip_bias, short_weight):
+    channels, block_len = conv_input.shape
+    shards = lax.axis_size("ctx")
+    owned = channels // shards
+    any_spec = pl.BlockSpec(memory_space=pl.ANY)
+    smem_spec = pl.BlockSpec(memory_space=pltpu.SMEM)
+    vmem_spec = pl.BlockSpec(memory_space=pltpu.VMEM)
+    return pl.pallas_call(
+        functools.partial(exchange_kernel, shards),
+        out_shape=(
+            jax.ShapeDtypeStruct((channels, block_len), jnp.bfloat16),
+            jax.ShapeDtypeStruct((channels, block_len), jnp.float32),
+        ),
+        in_specs=[any_spec] * 4 + [smem_spec] * 2,
+        out_specs=(vmem_spec, vmem_spec),
+        scratch_shapes=[
+            pltpu.VMEM((4, channels, LANES), jnp.bfloat16),
+            pltpu.VMEM((shards, 16, LANES), jnp.bfloat16),
+            pltpu.VMEM((shards, 16, LANES), jnp.bfloat16),
+            pltpu.VMEM((shards, 16, LANES), jnp.float32),
+            pltpu.VMEM((owned, 2, 2 * shards * SUBLANES, LANES), jnp.float32),
+            pltpu.VMEM((shards, 2 * owned, LANES), jnp.float32),
+            pltpu.VMEM((shards, 2 * owned, LANES), jnp.float32),
+            pltpu.SemaphoreType.DMA((4,)),
+            pltpu.SemaphoreType.DMA((shards,)),
+            pltpu.SemaphoreType.DMA((shards,)),
+            pltpu.SemaphoreType.DMA((shards,)),
+            pltpu.SemaphoreType.DMA((shards,)),
+        ],
+        compiler_params=pltpu.CompilerParams(collective_id=0, has_side_effects=True),
+    )(conv_input, gate_value, out_grad, long_filter, skip_bias, short_weight.T)
+
+
+def per_device(*args):
+    channels, block_len = args[0].shape
+    shards = lax.axis_size("ctx")
+    if block_len == LANES and shards == SUBLANES and channels == 4 * shards:
+        return exchange_device(*args)
+    return general_device(*args)
+
+
 def solution(mesh):
     placed = (
         P("ch", "ctx"),

time: 164 us -> 19.3 us (0.12)
  waiting for transfers between devices: 59.5 us -> 0 us
  blocking collectives: 53.7 us -> 0 us
  Pallas kernels: 0 us -> 16.4 us
  between operations: 14.2 us -> 0.65 us
  loops' own time: 11.5 us -> 0 us
  local copies, waits for them, and re-layouts: 9.46 us -> 1.91 us
  other arithmetic: 7.38 us -> 0 us
  matrix products: 6.9 us -> 0 us
    reduce_scatter x1 -> x0, waiting for transfers between devices: 56.6 us -> none  [per_device(): lax.psum_scatter(lag_part, 'ctx', scatter_dimension=1, tiled=True)]
    all_gather x2 -> x0, blocking collectives: 53.7 us -> none  [the longest x1 27.7 us: per_device(): piece = lax.all_gather(conv_grad, 'ctx', axis=1, tiled=True)]
    pallas_call x0 -> x1, Pallas kernels: none -> 16.4 us  [exchange_device(): pl.pallas_call(functools.partial(exchange_kernel, shards), out_shape=(jax...]
    another operation x9 -> x0, loops' own time: 11.5 us -> none  [the longest x8 5.92 us: step_one(): lax.cond(block_idx >= own_index, lambda inner: add_block(inner, grad_bloc...]
    dot_general x43 -> x0, matrix products: 6.9 us -> none  [the longest x17 2.44 us: split_dot(): jnp.dot(data, parts[1], preferred_element_type=jnp.float32)]
    dynamic_slice x8 -> x0, local copies, waits for them, and re-layouts: 5.29 us -> none  [per_device(): result, unused = lax.scan(step_one, init_state, (stacked, indices))]
    ppermute x1 -> x0, waiting for transfers between devices: 2.88 us -> none  [from_behind(): lax.ppermute(value, axis, [(source, source + steps) for source in range(i...]
    mul x4 -> x0, other arithmetic: 1.9 us -> none  [the longest x1 0.68 us: per_device(): lag_part = lag_acc[:, block_len:] * (1.0 / math.sqrt(shards * block_len))]
  transfers between devices with their start and end apart: 2 -> 0, of which waited for: 2 -> 0; matrix products, arithmetic and copies ran while one was open for 1% -> 0% of each run, Pallas kernels for 0% -> 0%
where the time goes in v1:
time: 19.3 us; the launch traced here: 19 us
  Pallas kernels  16.4 us (85%)
  local copies, waits for them, and re-layouts  1.91 us (10%)
  between operations  0.65 us (3%)
    pallas_call x1, Pallas kernels, exchange_device(): pl.pallas_call(functools.partial(exchange_kernel, shards), out_shape=(jax...  16.4 us
    unnamed x4, local copies, waits for them, and re-layouts  1.91 us

profile of v1, /device:TPU:0, one launch (start us, length us, event | category | flops | bytes accessed | tf_op | source)
XLA Modules:
  0.0 19.0 jit_solution(15356919168926587217)
XLA Ops:
  0.6 16.4 %shard_map.77 = (bf16[32,128]{1,0:T(8,128)(2,1)}, f32[32,128]{1,0:T(8,128)}) custom-call(bf16[32,128]{1,0:T(8,128)(2,1)} %input_ref.1, bf16[32,128]{1,0:T(8,128)(2,1)} %gate_ref.1, bf16[32,128]{1,0:T(8,128)(2,1)} %grad_ref.1, bf16[32,128]{1,0:T(8,128)(2,1)} %filter_ref.1, f32[32]{0:T(128)} %skip_ref.1, f32[3,32]{1,0:T(4,128)} %bitcast.1), custom_call_target="tpu_custom_call" | custom-call | tf_op jit(solution)/shard_map/pallas_call | solution.py:307
  17.0 0.0 copy-start
  17.0 1.3 %copy.10 = bf16[32,128]{1,0:T(8,128)(2,1)} copy(bf16[32,128]{1,0:T(8,128)(2,1)} %get-tuple-element.4) | data formatting | bytes 16384
  18.3 0.0 copy-done
  18.3 0.6 %copy.11 = f32[32,128]{1,0:T(8,128)} copy(f32[32,128]{1,0:T(8,128)S(1)} %copy-done) | data formatting | bytes 32768
Async XLA Ops:
  17.0 1.3 %copy-start = (f32[32,128]{1,0:T(8,128)S(1)}, f32[32,128]{1,0:T(8,128)}, u32[]{:S(2)}) copy-start(f32[32,128]{1,0:T(8,128)} %get-tuple-element.5) | copy-start | bytes 49156

commit v2 on v0

v2 whole, which is shorter than its diff:
```python
import functools
import math

import jax
import jax.numpy as jnp
from jax import lax
from jax.experimental import pallas as pl
from jax.experimental.pallas import tpu as pltpu
from jax.sharding import PartitionSpec as P

LANES = 128
GROUP = 8


def gather_kernel(
    shards,
    input_ref,
    gate_ref,
    grad_ref,
    filter_ref,
    skip_ref,
    short_ref,
    input_grad_ref,
    filter_grad_ref,
    local,
    skip_row,
    short_rows,
    grads,
    pairs,
    sums,
    halo,
    shifted,
    load_sem,
    grad_send,
    grad_recv,
    pair_send,
    pair_recv,
):
    me = lax.axis_index("ctx")
    channels = local.shape[1]
    taps = short_rows.shape[0]
    last = shards - 1

    barrier = pltpu.get_barrier_semaphore()

    @pl.loop(me + 1, shards)
    def _(peer):
        pl.semaphore_signal(
            barrier, inc=1, device_id={"ctx": peer}, device_id_type=pl.DeviceIdType.MESH
        )

    loads = [
        pltpu.make_async_copy(source, target, load_sem.at[slot])
        for slot, (source, target) in enumerate(
            (
                (gate_ref, local.at[0]),
                (grad_ref, local.at[1]),
                (filter_ref, local.at[2]),
                (input_ref, local.at[3]),
                (skip_ref, skip_row),
                (short_ref, short_rows),
            )
        )
    ]
    for load in loads:
        load.start()
    grads[shards] = jnp.zeros((channels, LANES), jnp.bfloat16)
    sums[...] = jnp.zeros_like(sums)
    halo[...] = jnp.zeros_like(halo)
    shifted[...] = jnp.zeros_like(shifted)
    lane = lax.broadcasted_iota(jnp.int32, (LANES, LANES), 1)
    depth = lax.broadcasted_iota(jnp.int32, (LANES, LANES), 0)
    mirror = jnp.where(lane + depth == LANES - 1, 1.0, 0.0).astype(jnp.bfloat16)
    ahead = lane + depth >= LANES - 1

    def grad_copy(source, target):
        return pltpu.make_async_remote_copy(
            src_ref=grads.at[source],
            dst_ref=grads.at[source],
            send_sem=grad_send.at[target],
            recv_sem=grad_recv.at[source],
            device_id={"ctx": target},
            device_id_type=pl.DeviceIdType.MESH,
        )

    def pair_copy(source, target):
        return pltpu.make_async_remote_copy(
            src_ref=pairs.at[source],
            dst_ref=pairs.at[source],
            send_sem=pair_send.at[target],
            recv_sem=pair_recv.at[source],
            device_id={"ctx": target},
            device_id_type=pl.DeviceIdType.MESH,
        )

    loads[0].wait()
    loads[1].wait()
    grads[me] = (local[0].astype(jnp.float32) * local[1].astype(jnp.float32)).astype(jnp.bfloat16)

    @pl.when(me > 0)
    def _():
        pl.semaphore_wait(barrier, me)

    @pl.loop(0, me)
    def _(peer):
        grad_copy(me, peer).start()

    loads[2].wait()
    loads[3].wait()
    both = jnp.concatenate([local[2], local[3]], axis=0)
    pairs[me] = jnp.dot(both, mirror, preferred_element_type=jnp.float32).astype(jnp.bfloat16)

    @pl.loop(0, jnp.minimum(me, shards - me))
    def _(peer):
        pair_copy(me, peer).start()

    loads[4].wait()
    loads[5].wait()
    rows8 = lax.broadcasted_iota(jnp.int32, (2 * GROUP, LANES), 0) % GROUP
    lane_row = lax.broadcasted_iota(jnp.int32, (channels, LANES), 1)

    def step(lag, carry):
        now = me + lag
        after = now + 1

        @pl.when(after < shards)
        def _():
            grad_copy(after, after).wait_recv()

        @pl.when(jnp.logical_and(after < shards, after < shards - me))
        def _():
            pair_copy(me, after).start()

        @pl.when(lag != me)
        def _():
            pair_copy(lag, lag).wait_recv()

        grad_now = grads[now].astype(jnp.float32)
        grad_next = grads[after].astype(jnp.float32)
        pair = pairs[lag]
        plain = jnp.dot(pair[:channels], mirror, preferred_element_type=jnp.float32)
        halo[0] += plain * grad_next
        turn = plain
        for tap in range(1, taps - 1):
            turn = pltpu.roll(plain, tap, 1)
            halo[tap] += jnp.where(lane_row < tap, shifted[tap], turn) * grad_next
            shifted[tap] = turn
        pair = pair.astype(jnp.float32)
        for group in range(channels // GROUP):
            at = slice(group * GROUP, (group + 1) * GROUP)
            stack = jnp.concatenate([pair[:channels][at], pair[channels:][at]], axis=0)
            weights, hankel = [], []
            for item in range(GROUP):
                row = slice(group * GROUP + item, group * GROUP + item + 1)
                weights.append(jnp.where(rows8 == item, stack, 0.0).astype(jnp.bfloat16))
                mixed = jnp.where(
                    ahead,
                    jnp.broadcast_to(grad_now[row], (LANES, LANES)),
                    jnp.broadcast_to(grad_next[row], (LANES, LANES)),
                )
                hankel.append(
                    pltpu.roll(mixed, 1, 1, stride=1, stride_axis=0).astype(jnp.bfloat16)
                )
            sums[group] += jnp.dot(
                jnp.concatenate(weights, axis=1),
                jnp.concatenate(hankel, axis=0),
                preferred_element_type=jnp.float32,
            )
        return carry

    lax.fori_loop(0, shards - me, step, 0)

    wide = skip_row.shape[1]
    eye = lax.broadcasted_iota(jnp.int32, (channels, wide), 0) == lax.broadcasted_iota(
        jnp.int32, (channels, wide), 1
    )

    def column(row):
        return jnp.sum(jnp.where(eye, row, 0.0), axis=1, keepdims=True)

    skip = column(skip_row[...])
    own = grads[me].astype(jnp.float32)
    ahead_grad = grads[me + 1].astype(jnp.float32)

    def rounded(value):
        return value.astype(jnp.bfloat16).astype(jnp.float32)

    groups = channels // GROUP
    mid = rounded(
        jnp.concatenate([sums[group, :GROUP] for group in range(groups)], axis=0) + skip * own
    )
    scale = 1.0 / math.sqrt(shards * LANES)
    filter_grad_ref[...] = scale * jnp.concatenate(
        [sums[group, GROUP:] for group in range(groups)], axis=0
    )
    edge = [
        rounded(
            jnp.sum(halo[tap], axis=1, keepdims=True) + skip * ahead_grad[:, tap : tap + 1]
        )
        for tap in range(taps - 1)
    ]
    total = column(short_rows[0:1, :]) * mid
    for tap in range(1, taps):
        moved = pltpu.roll(mid, LANES - tap, 1)
        for reach in range(tap):
            moved = jnp.where(lane_row == LANES - tap + reach, edge[reach], moved)
        total = total + column(short_rows[tap : tap + 1, :]) * moved
    input_grad_ref[...] = total.astype(jnp.bfloat16)

    @pl.loop(0, me)
    def _(peer):
        grad_copy(me, peer).wait_send()

    @pl.loop(0, shards - me)
    def _(peer):
        @pl.when(peer != me)
        def _():
            pair_copy(me, peer).wait_send()


def per_device(conv_input, gate_value, out_grad, long_filter, skip_bias, short_weight):
    channels, block_len = conv_input.shape
    taps = short_weight.shape[1]
    shards = lax.axis_size("ctx")
    any_spec = pl.BlockSpec(memory_space=pl.ANY)
    vmem_spec = pl.BlockSpec(memory_space=pltpu.VMEM)
    return pl.pallas_call(
        functools.partial(gather_kernel, shards),
        out_shape=(
            jax.ShapeDtypeStruct((channels, block_len), jnp.bfloat16),
            jax.ShapeDtypeStruct((channels, block_len), jnp.float32),
        ),
        in_specs=[any_spec] * 6,
        out_specs=(vmem_spec, vmem_spec),
        scratch_shapes=[
            pltpu.VMEM((4, channels, LANES), jnp.bfloat16),
            pltpu.VMEM((1, channels), jnp.float32),
            pltpu.VMEM((taps, channels), jnp.float32),
            pltpu.VMEM((shards + 1, channels, LANES), jnp.bfloat16),
            pltpu.VMEM((shards, 2 * channels, LANES), jnp.bfloat16),
            pltpu.VMEM((channels // GROUP, 2 * GROUP, LANES), jnp.float32),
            pltpu.VMEM((taps - 1, channels, LANES), jnp.float32),
            pltpu.VMEM((taps - 1, channels, LANES), jnp.float32),
            pltpu.SemaphoreType.DMA((6,)),
            pltpu.SemaphoreType.DMA((shards,)),
            pltpu.SemaphoreType.DMA((shards,)),
            pltpu.SemaphoreType.DMA((shards,)),
            pltpu.SemaphoreType.DMA((shards,)),
        ],
        compiler_params=pltpu.CompilerParams(collective_id=0, has_side_effects=True),
    )(
        conv_input,
        gate_value,
        out_grad,
        long_filter,
        skip_bias.reshape(1, channels),
        short_weight.T,
    )


def solution(mesh):
    placed = (
        P("ch", "ctx"),
        P("ch", "ctx"),
        P("ch", "ctx"),
        P("ch", "ctx"),
        P("ch"),
        P("ch", None),
    )
    return jax.shard_map(
        per_device,
        mesh=mesh,
        in_specs=placed,
        out_specs=(P("ch", "ctx"), P("ch", "ctx")),
        check_vma=False,
    )
```

time: 164 us -> 15.4 us (0.09)
  the two profiles are of different devices: /device:TPU:0 before, /device:TPU:16 now
where the time goes in v2:
time: 15.4 us; the launch traced here: 15.2 us
  Pallas kernels  12.7 us (82%)
  local copies, waits for them, and re-layouts  1.91 us (12%)
  between operations  0.65 us (4%)
    pallas_call x1, Pallas kernels, per_device(): pl.pallas_call(functools.partial(gather_kernel, shards), out_shape=(jax.S...  12.7 us
    unnamed x4, local copies, waits for them, and re-layouts  1.91 us

profile of v2, /device:TPU:16, one launch (start us, length us, event | category | flops | bytes accessed | tf_op | source)
XLA Modules:
  0.0 15.2 jit_solution(17937350725528706015)
XLA Ops:
  0.6 12.7 %shard_map.77 = (bf16[32,128]{1,0:T(8,128)(2,1)}, f32[32,128]{1,0:T(8,128)}) custom-call(bf16[32,128]{1,0:T(8,128)(2,1)} %input_ref.1, bf16[32,128]{1,0:T(8,128)(2,1)} %gate_ref.1, bf16[32,128]{1,0:T(8,128)(2,1)} %grad_ref.1, bf16[32,128]{1,0:T(8,128)(2,1)} %filter_ref.1, f32[1,32]{1,0:T(1,128)} %bitcast.3, f32[3,32]{1,0:T(4,128)} %bitcast.2), custom_call_target="tpu_custom_call" | custom-call | tf_op jit(solution)/shard_map/pallas_call | solution.py:227
  13.3 0.0 copy-start
  13.3 1.3 %copy.10 = bf16[32,128]{1,0:T(8,128)(2,1)} copy(bf16[32,128]{1,0:T(8,128)(2,1)} %get-tuple-element.4) | data formatting | bytes 16384
  14.6 0.0 copy-done
  14.6 0.6 %copy.11 = f32[32,128]{1,0:T(8,128)} copy(f32[32,128]{1,0:T(8,128)S(1)} %copy-done) | data formatting | bytes 32768
Async XLA Ops:
  13.3 1.3 %copy-start = (f32[32,128]{1,0:T(8,128)S(1)}, f32[32,128]{1,0:T(8,128)}, u32[]{:S(2)}) copy-start(f32[32,128]{1,0:T(8,128)} %get-tuple-element.5) | copy-start | bytes 49156

commit v3 on v2

--- a/solution.py
+++ b/solution.py
@@ -10,6 +10,7 @@
 
 LANES = 128
 GROUP = 8
+EARLY = 4
 
 
 def gather_kernel(
@@ -35,19 +36,12 @@
     grad_recv,
     pair_send,
     pair_recv,
+    entered,
 ):
     me = lax.axis_index("ctx")
     channels = local.shape[1]
     taps = short_rows.shape[0]
     last = shards - 1
-
-    barrier = pltpu.get_barrier_semaphore()
-
-    @pl.loop(me + 1, shards)
-    def _(peer):
-        pl.semaphore_signal(
-            barrier, inc=1, device_id={"ctx": peer}, device_id_type=pl.DeviceIdType.MESH
-        )
 
     loads = [
         pltpu.make_async_copy(source, target, load_sem.at[slot])
@@ -64,6 +58,24 @@
     ]
     for load in loads:
         load.start()
+    barrier = pltpu.get_barrier_semaphore()
+
+    @pl.loop(me + 1, shards)
+    def _(peer):
+        pl.semaphore_signal(
+            barrier, inc=1, device_id={"ctx": peer}, device_id_type=pl.DeviceIdType.MESH
+        )
+
+    @pl.when(me > 0)
+    def _():
+        pl.semaphore_wait(barrier, me)
+
+    @pl.loop(0, jnp.minimum(me, shards - me))
+    def _(peer):
+        pl.semaphore_signal(
+            entered.at[me], inc=1, device_id={"ctx": peer}, device_id_type=pl.DeviceIdType.MESH
+        )
+
     grads[shards] = jnp.zeros((channels, LANES), jnp.bfloat16)
     sums[...] = jnp.zeros_like(sums)
     halo[...] = jnp.zeros_like(halo)
@@ -99,11 +111,7 @@
 
     @pl.when(me > 0)
     def _():
-        pl.semaphore_wait(barrier, me)
-
-    @pl.loop(0, me)
-    def _(peer):
-        grad_copy(me, peer).start()
+        grad_copy(me, 0).start()
 
     loads[2].wait()
     loads[3].wait()
@@ -114,6 +122,20 @@
     def _(peer):
         pair_copy(me, peer).start()
 
+    @pl.loop(1, me)
+    def _(peer):
+        grad_copy(me, peer).start()
+
+    def push_up(peer):
+        @pl.when(peer < shards - me)
+        def _():
+            pl.semaphore_wait(entered.at[peer], 1)
+            pair_copy(me, peer).start()
+
+    @pl.loop(me + 1, me + 1 + EARLY)
+    def _(peer):
+        push_up(peer)
+
     loads[4].wait()
     loads[5].wait()
     rows8 = lax.broadcasted_iota(jnp.int32, (2 * GROUP, LANES), 0) % GROUP
@@ -127,9 +149,7 @@
         def _():
             grad_copy(after, after).wait_recv()
 
-        @pl.when(jnp.logical_and(after < shards, after < shards - me))
-        def _():
-            pair_copy(me, after).start()
+        push_up(after + EARLY)
 
         @pl.when(lag != me)
         def _():
@@ -227,8 +247,8 @@
     return pl.pallas_call(
         functools.partial(gather_kernel, shards),
         out_shape=(
-            jax.ShapeDtypeStruct((channels, block_len), jnp.bfloat16),
-            jax.ShapeDtypeStruct((channels, block_len), jnp.float32),
+            pltpu.VMEM((channels, block_len), jnp.bfloat16),
+            pltpu.VMEM((channels, block_len), jnp.float32),
         ),
         in_specs=[any_spec] * 6,
         out_specs=(vmem_spec, vmem_spec),
@@ -246,8 +266,12 @@
             pltpu.SemaphoreType.DMA((shards,)),
             pltpu.SemaphoreType.DMA((shards,)),
             pltpu.SemaphoreType.DMA((shards,)),
+            pltpu.SemaphoreType.REGULAR((shards,)),
         ],
-        compiler_params=pltpu.CompilerParams(collective_id=0, has_side_effects=True),
+        compiler_params=pltpu.CompilerParams(
+            collective_id=0,
+            has_side_effects=True,
+        ),
     )(
         conv_input,
         gate_value,

time: 15.4 us -> 12.8 us (0.83)
  the two profiles are of different devices: /device:TPU:16 before, /device:TPU:0 now
where the time goes in v3:
time: 12.8 us; the launch traced here: 12.6 us
  Pallas kernels  10.7 us (84%)
  local copies, waits for them, and re-layouts  1.21 us (9%)
  between operations  0.64 us (5%)
    pallas_call x1, Pallas kernels, per_device(): pl.pallas_call(functools.partial(gather_kernel, shards), out_shape=(pltpu...  10.7 us
    unnamed x2, local copies, waits for them, and re-layouts  1.21 us

profile of v3, /device:TPU:0, one launch (start us, length us, event | category | flops | bytes accessed | tf_op | source)
XLA Modules:
  0.0 12.6 jit_solution(6220270353542939224)
XLA Ops:
  0.6 10.7 %shard_map.77 = (bf16[32,128]{1,0:T(8,128)(2,1)S(1)}, f32[32,128]{1,0:T(8,128)S(1)}) custom-call(bf16[32,128]{1,0:T(8,128)(2,1)} %input_ref.1, bf16[32,128]{1,0:T(8,128)(2,1)} %gate_ref.1, bf16[32,128]{1,0:T(8,128)(2,1)} %grad_ref.1, bf16[32,128]{1,0:T(8,128)(2,1)} %filter_ref.1, f32[1,32]{1,0:T(1,128)} %bitcast.3, f32[3,32]{1,0:T(4,128)} %bitcast.2), custom_call_target="tpu_custom_call" | custom-call | tf_op jit(solution)/shard_map/pallas_call | solution.py:247
  11.4 0.6 %copy.10 = bf16[32,128]{1,0:T(8,128)(2,1)} copy(bf16[32,128]{1,0:T(8,128)(2,1)S(1)} %get-tuple-element.2) | data formatting | bytes 16384
  12.0 0.6 %copy.11 = f32[32,128]{1,0:T(8,128)} copy(f32[32,128]{1,0:T(8,128)S(1)} %get-tuple-element.3) | data formatting | bytes 32768

commit v4 on v3

--- a/solution.py
+++ b/solution.py
@@ -238,13 +238,39 @@
             pair_copy(me, peer).wait_send()
 
 
+def place_kernel(small_ref, wide_ref, small_out, wide_out, sem):
+    copies = [
+        pltpu.make_async_copy(source, target, sem.at[slot])
+        for slot, (source, target) in enumerate(((wide_ref, wide_out), (small_ref, small_out)))
+    ]
+    for copy in copies:
+        copy.start()
+    for copy in copies:
+        copy.wait()
+
+
+def placed_copy(small, wide):
+    any_spec = pl.BlockSpec(memory_space=pl.ANY)
+    vmem_spec = pl.BlockSpec(memory_space=pltpu.VMEM)
+    return pl.pallas_call(
+        place_kernel,
+        out_shape=(
+            jax.ShapeDtypeStruct(small.shape, small.dtype),
+            jax.ShapeDtypeStruct(wide.shape, wide.dtype),
+        ),
+        in_specs=[vmem_spec] * 2,
+        out_specs=(any_spec, any_spec),
+        scratch_shapes=[pltpu.SemaphoreType.DMA((2,))],
+    )(*(pltpu.with_memory_space_constraint(value, pltpu.VMEM) for value in (small, wide)))
+
+
 def per_device(conv_input, gate_value, out_grad, long_filter, skip_bias, short_weight):
     channels, block_len = conv_input.shape
     taps = short_weight.shape[1]
     shards = lax.axis_size("ctx")
     any_spec = pl.BlockSpec(memory_space=pl.ANY)
     vmem_spec = pl.BlockSpec(memory_space=pltpu.VMEM)
-    return pl.pallas_call(
+    results = pl.pallas_call(
         functools.partial(gather_kernel, shards),
         out_shape=(
             pltpu.VMEM((channels, block_len), jnp.bfloat16),
@@ -280,6 +306,7 @@
         skip_bias.reshape(1, channels),
         short_weight.T,
     )
+    return placed_copy(*results)
 
 
 def solution(mesh):

time: 12.8 us -> 12.2 us (0.953)
  local copies, waits for them, and re-layouts: 1.21 us -> 0 us
  Pallas kernels: 10.7 us -> 11.3 us
    unnamed x2 -> x0, local copies, waits for them, and re-layouts: 1.21 us -> none
    pallas_call x0 -> x1, Pallas kernels: none -> 0.63 us  [placed_copy(): pl.pallas_call(place_kernel, out_shape=(jax.ShapeDtypeStruct(small.shape,...]
where the time goes in v4:
time: 12.2 us; the launch traced here: 12 us
  Pallas kernels  11.3 us (93%)
  between operations  0.64 us (5%)
    pallas_call x1, Pallas kernels, per_device(): pl.pallas_call(functools.partial(gather_kernel, shards), out_shape=(pltpu...  10.7 us
    pallas_call x1, Pallas kernels, placed_copy(): pl.pallas_call(place_kernel, out_shape=(jax.ShapeDtypeStruct(small.shape,...  0.63 us

profile of v4, /device:TPU:0, one launch (start us, length us, event | category | flops | bytes accessed | tf_op | source)
XLA Modules:
  0.0 12.0 jit_solution(3457764465356852620)
XLA Ops:
  0.6 10.7 %shard_map.77 = (bf16[32,128]{1,0:T(8,128)(2,1)S(1)}, f32[32,128]{1,0:T(8,128)S(1)}) custom-call(bf16[32,128]{1,0:T(8,128)(2,1)} %input_ref.1, bf16[32,128]{1,0:T(8,128)(2,1)} %gate_ref.1, bf16[32,128]{1,0:T(8,128)(2,1)} %grad_ref.1, bf16[32,128]{1,0:T(8,128)(2,1)} %filter_ref.1, f32[1,32]{1,0:T(1,128)} %bitcast.3, f32[3,32]{1,0:T(4,128)} %bitcast.2), custom_call_target="tpu_custom_call" | custom-call | tf_op jit(solution)/shard_map/pallas_call | solution.py:273
  11.4 0.6 %shard_map.78 = (bf16[32,128]{1,0:T(8,128)(2,1)}, f32[32,128]{1,0:T(8,128)}) custom-call(bf16[32,128]{1,0:T(8,128)(2,1)S(1)} %get-tuple-element.4.small_ref, f32[32,128]{1,0:T(8,128)S(1)} %get-tuple-element.5.wide_ref), custom_call_target="tpu_custom_call" | custom-call | tf_op jit(solution)/shard_map/pallas_call | solution.py:255

commit v5 on v4

--- a/solution.py
+++ b/solution.py
@@ -83,7 +83,7 @@
     lane = lax.broadcasted_iota(jnp.int32, (LANES, LANES), 1)
     depth = lax.broadcasted_iota(jnp.int32, (LANES, LANES), 0)
     mirror = jnp.where(lane + depth == LANES - 1, 1.0, 0.0).astype(jnp.bfloat16)
-    ahead = lane + depth >= LANES - 1
+    own_part = lane <= depth
 
     def grad_copy(source, target):
         return pltpu.make_async_remote_copy(
@@ -141,46 +141,56 @@
     rows8 = lax.broadcasted_iota(jnp.int32, (2 * GROUP, LANES), 0) % GROUP
     lane_row = lax.broadcasted_iota(jnp.int32, (channels, LANES), 1)
 
+    wide = skip_row.shape[1]
+    eye = lax.broadcasted_iota(jnp.int32, (channels, wide), 0) == lax.broadcasted_iota(
+        jnp.int32, (channels, wide), 1
+    )
+
+    def column(row):
+        return jnp.sum(jnp.where(eye, row, 0.0), axis=1, keepdims=True)
+
+    skip = column(skip_row[...])
+    short = [column(short_rows[tap : tap + 1, :]) for tap in range(taps)]
+
     def step(lag, carry):
         now = me + lag
-        after = now + 1
-
-        @pl.when(after < shards)
+
+        @pl.when(lag > 0)
         def _():
-            grad_copy(after, after).wait_recv()
-
-        push_up(after + EARLY)
+            grad_copy(now, now).wait_recv()
+            push_up(now + EARLY)
 
         @pl.when(lag != me)
         def _():
             pair_copy(lag, lag).wait_recv()
 
         grad_now = grads[now].astype(jnp.float32)
-        grad_next = grads[after].astype(jnp.float32)
-        pair = pairs[lag]
-        plain = jnp.dot(pair[:channels], mirror, preferred_element_type=jnp.float32)
-        halo[0] += plain * grad_next
-        turn = plain
+        pair = pairs[lag].astype(jnp.float32)
+        before = pairs[jnp.maximum(lag - 1, 0)].astype(jnp.float32)
+        before = jnp.where(lag > 0, before, 0.0)
+        plain = jnp.dot(
+            before[:channels].astype(jnp.bfloat16), mirror, preferred_element_type=jnp.float32
+        )
+        halo[0] += plain * grad_now
         for tap in range(1, taps - 1):
             turn = pltpu.roll(plain, tap, 1)
-            halo[tap] += jnp.where(lane_row < tap, shifted[tap], turn) * grad_next
+            halo[tap] += jnp.where(lane_row < tap, shifted[tap], turn) * grad_now
             shifted[tap] = turn
-        pair = pair.astype(jnp.float32)
         for group in range(channels // GROUP):
             at = slice(group * GROUP, (group + 1) * GROUP)
-            stack = jnp.concatenate([pair[:channels][at], pair[channels:][at]], axis=0)
+            stacks = [
+                jnp.concatenate([source[:channels][at], source[channels:][at]], axis=0)
+                for source in (pair, before)
+            ]
             weights, hankel = [], []
             for item in range(GROUP):
                 row = slice(group * GROUP + item, group * GROUP + item + 1)
-                weights.append(jnp.where(rows8 == item, stack, 0.0).astype(jnp.bfloat16))
-                mixed = jnp.where(
-                    ahead,
-                    jnp.broadcast_to(grad_now[row], (LANES, LANES)),
-                    jnp.broadcast_to(grad_next[row], (LANES, LANES)),
+                turned = pltpu.roll(
+                    jnp.broadcast_to(grad_now[row], (LANES, LANES)), 1, 1, stride=1, stride_axis=0
                 )
-                hankel.append(
-                    pltpu.roll(mixed, 1, 1, stride=1, stride_axis=0).astype(jnp.bfloat16)
-                )
+                for stack, kept in zip(stacks, (own_part, ~own_part)):
+                    weights.append(jnp.where(rows8 == item, stack, 0.0).astype(jnp.bfloat16))
+                    hankel.append(jnp.where(kept, turned, 0.0).astype(jnp.bfloat16))
             sums[group] += jnp.dot(
                 jnp.concatenate(weights, axis=1),
                 jnp.concatenate(hankel, axis=0),
@@ -190,15 +200,6 @@
 
     lax.fori_loop(0, shards - me, step, 0)
 
-    wide = skip_row.shape[1]
-    eye = lax.broadcasted_iota(jnp.int32, (channels, wide), 0) == lax.broadcasted_iota(
-        jnp.int32, (channels, wide), 1
-    )
-
-    def column(row):
-        return jnp.sum(jnp.where(eye, row, 0.0), axis=1, keepdims=True)
-
-    skip = column(skip_row[...])
     own = grads[me].astype(jnp.float32)
     ahead_grad = grads[me + 1].astype(jnp.float32)
 
@@ -219,12 +220,12 @@
         )
         for tap in range(taps - 1)
     ]
-    total = column(short_rows[0:1, :]) * mid
+    total = short[0] * mid
     for tap in range(1, taps):
         moved = pltpu.roll(mid, LANES - tap, 1)
         for reach in range(tap):
             moved = jnp.where(lane_row == LANES - tap + reach, edge[reach], moved)
-        total = total + column(short_rows[tap : tap + 1, :]) * moved
+        total = total + short[tap] * moved
     input_grad_ref[...] = total.astype(jnp.bfloat16)
 
     @pl.loop(0, me)

time: 12.2 us -> 11.9 us (0.975)
  Pallas kernels: 11.3 us -> 11.1 us
    pallas_call x1, Pallas kernels: 10.7 us -> 10.4 us  [per_device(): pl.pallas_call(functools.partial(gather_kernel, shards), out_shape=(pltpu...]
where the time goes in v5:
time: 11.9 us; the launch traced here: 11.7 us
  Pallas kernels  11.1 us (93%)
  between operations  0.64 us (5%)
    pallas_call x1, Pallas kernels, per_device(): pl.pallas_call(functools.partial(gather_kernel, shards), out_shape=(pltpu...  10.4 us
    pallas_call x1, Pallas kernels, placed_copy(): pl.pallas_call(place_kernel, out_shape=(jax.ShapeDtypeStruct(small.shape,...  0.63 us

profile of v5, /device:TPU:0, one launch (start us, length us, event | category | flops | bytes accessed | tf_op | source)
XLA Modules:
  0.0 11.7 jit_solution(17155516035168373790)
XLA Ops:
  0.6 10.4 %shard_map.77 = (bf16[32,128]{1,0:T(8,128)(2,1)S(1)}, f32[32,128]{1,0:T(8,128)S(1)}) custom-call(bf16[32,128]{1,0:T(8,128)(2,1)} %input_ref.1, bf16[32,128]{1,0:T(8,128)(2,1)} %gate_ref.1, bf16[32,128]{1,0:T(8,128)(2,1)} %grad_ref.1, bf16[32,128]{1,0:T(8,128)(2,1)} %filter_ref.1, f32[1,32]{1,0:T(1,128)} %bitcast.3, f32[3,32]{1,0:T(4,128)} %bitcast.2), custom_call_target="tpu_custom_call" | custom-call | tf_op jit(solution)/shard_map/pallas_call | solution.py:274
  11.1 0.6 %shard_map.78 = (bf16[32,128]{1,0:T(8,128)(2,1)}, f32[32,128]{1,0:T(8,128)}) custom-call(bf16[32,128]{1,0:T(8,128)(2,1)S(1)} %get-tuple-element.4.small_ref, f32[32,128]{1,0:T(8,128)S(1)} %get-tuple-element.5.wide_ref), custom_call_target="tpu_custom_call" | custom-call | tf_op jit(solution)/shard_map/pallas_call | solution.py:256
